TPU v7x, 32 devices: a whole 2x2x4 slice. The times are simulated.
32 devices in a mesh: sx: 8 (over y, x, core), sy: 4 (over z).
Axes of the slice: x: 2, y: 2, z: 4, core: 2. Of those that a mesh axis runs over, the one named last changes fastest.
Arguments:
- schur_x: float32 [16, 4, 512, 512], P('sx', 'sy'), may hold values from -1 to 5, as said below
- schur_y: float32 [8, 8, 512, 512], P('sx', 'sy'), may hold values from -1 to 5, as said below
- residual_x: float32 [16, 4, 32, 512], P('sx', 'sy'), may hold values from -36 to 36
- residual_y: float32 [8, 8, 32, 512], P('sx', 'sy'), may hold values from -36 to 36
- basis_x: float32 [16, 4, 6, 512], P('sx', 'sy'), may hold values from -0.9 to 0.9
- basis_y: float32 [8, 8, 6, 512], P('sx', 'sy'), may hold values from -0.9 to 0.9
- couple_x: float32 [8, 4, 6, 6], P('sx', 'sy'), may hold values from -0.3 to 0.1
- couple_y: float32 [8, 4, 6, 6], P('sx', 'sy'), may hold values from -0.3 to 0.1
- coarse_shift: float32 [8, 4, 6], P('sx', 'sy'), may hold values from 0.05 to 0.5
Outputs:
- average_x: float32 [16, 4, 32, 512], P('sx', 'sy')
- average_y: float32 [8, 8, 32, 512], P('sx', 'sy')
- coarse_values: float32 [8, 4, 6, 32], P('sx', 'sy')
Inputs may be any that keep to these rules, and one draw needn't show every extreme that they name: `schur_x`: every block is symmetric positive definite. `schur_y`: every block is symmetric positive definite.
All inputs are finite; a program needn't handle non-finite values.
Results may differ from a plain program's by a relative error of at most 0.0003.
Values sent between devices are 32-bit elements; how exact they have to be, the bound alone decides.
No kernel may reach another device: no remote copies, remote signals or barrier semaphores. Data moves between devices by JAX's collectives and lax.ppermute only.
A program may use at most 128 MiB of HBM per device.

v0:
```python
import jax
import jax.numpy as jnp
from jax import lax
from jax.sharding import PartitionSpec as P

CITERS = 8
HIGH = lax.Precision.HIGHEST


def shifted(array, axis, by):
    count = lax.axis_size(axis)
    pairs = [(i, i + by) for i in range(count) if 0 <= i + by < count]
    return lax.ppermute(array, axis, pairs)


def with_halo(cells, sides, width):
    for axis, dim in sides:
        count = lax.axis_size(axis)
        ends = count - 1
        head = lax.slice_in_dim(cells, 0, width, axis=dim)
        tail = lax.slice_in_dim(cells, cells.shape[dim] - width, cells.shape[dim], axis=dim)
        cells = jnp.concatenate(
            [
                lax.ppermute(tail, axis, [(i, (i + 1) % count) for i in range(ends)]),
                cells,
                lax.ppermute(head, axis, [((i + 1) % count, i) for i in range(ends)]),
            ],
            axis=dim,
        )
    return cells


def face_average(s_low, s_high, r_low, r_high):
    summed = s_low + s_high
    factor = jnp.linalg.cholesky(summed)
    right_side = jnp.dot(s_low, r_low.T, precision=HIGH) + jnp.dot(s_high, r_high.T, precision=HIGH)
    forward = jax.scipy.linalg.solve_triangular(factor, right_side, lower=True)
    solved = jax.scipy.linalg.solve_triangular(factor, forward, lower=True, trans=1)
    return solved.T


def shards(
    schur_x, schur_y, residual_x, residual_y, basis_x, basis_y, couple_x, couple_y, coarse_shift
):
    row_index = lax.axis_index("sx")
    row_count = lax.axis_size("sx")
    col_index = lax.axis_index("sy")
    col_count = lax.axis_size("sy")
    link_x = couple_x[0, 0] * (row_index > 0).astype(jnp.float32)
    link_y = couple_y[0, 0] * (col_index > 0).astype(jnp.float32)
    above_x = shifted((schur_x[0, 0], residual_x[0, 0], link_x), "sx", -1)
    above_y = shifted((schur_y[0, 0], residual_y[0, 0], link_y), "sy", -1)
    upper_x = face_average(schur_x[1, 0], above_x[0], residual_x[1, 0], above_x[1])
    upper_y = face_average(schur_y[0, 1], above_y[0], residual_y[0, 1], above_y[1])
    upper_x = jnp.where(row_index == row_count - 1, residual_x[1, 0], upper_x)
    upper_y = jnp.where(col_index == col_count - 1, residual_y[0, 1], upper_y)
    lower_x = shifted(upper_x, "sx", 1)
    lower_y = shifted(upper_y, "sy", 1)
    next_x = above_x[2]
    next_y = above_y[2]
    lower_x = jnp.where(row_index == 0, residual_x[0, 0], lower_x)
    upper_x = jnp.where(row_index == row_count - 1, residual_x[1, 0], upper_x)
    lower_y = jnp.where(col_index == 0, residual_y[0, 0], lower_y)
    upper_y = jnp.where(col_index == col_count - 1, residual_y[0, 1], upper_y)
    rhs_coarse = jnp.einsum("spf,srf->pr", basis_x[:, 0], residual_x[:, 0], precision=HIGH)
    rhs_coarse = rhs_coarse + jnp.einsum("spf,srf->pr", basis_y[0], residual_y[0], precision=HIGH)
    diagonal = (
        jnp.sum(jnp.abs(link_x), axis=0)
        + jnp.sum(jnp.abs(next_x), axis=1)
        + jnp.sum(jnp.abs(link_y), axis=0)
        + jnp.sum(jnp.abs(next_y), axis=1)
        + coarse_shift[0, 0]
    )
    coarse = jnp.zeros_like(rhs_coarse)
    remain = rhs_coarse

    def squares(values):
        return lax.psum(jnp.sum(values * values, axis=0), ("sx", "sy"))

    direction = rhs_coarse
    norm_now = squares(remain)
    for sweep_index in range(CITERS):
        padded = with_halo(direction[None, None], (("sx", 0), ("sy", 1)), 1)
        image = diagonal[:, None] * direction
        image = image + jnp.dot(link_x.T, padded[0, 1], precision=HIGH)
        image = image + jnp.dot(next_x, padded[2, 1], precision=HIGH)
        image = image + jnp.dot(link_y.T, padded[1, 0], precision=HIGH)
        image = image + jnp.dot(next_y, padded[1, 2], precision=HIGH)
        curve = lax.psum(jnp.sum(direction * image, axis=0), ("sx", "sy"))
        alpha = norm_now / curve
        coarse = coarse + alpha * direction
        remain = remain - alpha * image
        norm_next = squares(remain)
        direction = remain + norm_next / norm_now * direction
        norm_now = norm_next
    lift_x = jnp.einsum("pr,spf->srf", coarse, basis_x[:, 0], precision=HIGH)
    lift_y = jnp.einsum("pr,spf->srf", coarse, basis_y[0], precision=HIGH)
    out_x = (jnp.stack([lower_x, upper_x], axis=0) + lift_x)[:, None]
    out_y = (jnp.stack([lower_y, upper_y], axis=0) + lift_y)[None]
    return (out_x, out_y, coarse[None, None])


def solution(mesh):
    placed = (
        P("sx", "sy", None, None),
        P("sx", "sy", None, None),
        P("sx", "sy", None, None),
        P("sx", "sy", None, None),
        P("sx", "sy", None, None),
        P("sx", "sy", None, None),
        P("sx", "sy", None, None),
        P("sx", "sy", None, None),
        P("sx", "sy", None),
    )
    return jax.shard_map(
        shards,
        mesh=mesh,
        in_specs=placed,
        out_specs=(P("sx", "sy", None, None), P("sx", "sy", None, None), P("sx", "sy", None, None)),
        check_vma=False,
    )
```

profile of v0, /device:TPU:1, one launch (start us, length us, event | category | flops | bytes accessed | tf_op | source)
XLA Modules:
  0.0 1094.7 jit_solution(9684428249556823600)
XLA Ops:
  5.6 4.5 collective-permute-start.5
  19.8 4.6 collective-permute-start.7
  27.0 40.4 %all-reduce.1 = (f32[32]{0:T(128)S(1)}, f32[32]{0:T(128)S(1)}) all-reduce(f32[32]{0:T(128)S(1)} %get-tuple-element.45, f32[32]{0:T(128)S(1)} %get-tuple-element.44), channel_id=1, replica_groups=mesh['sx'=8,'sy'=4] {'sx','sy'}, use_global_device_ids=true, to_apply=%region_9.13 | all-reduce | flops 64 | bytes 512 | tf_op jit(solution)/shard_map/psum | solution.py:78
  67.5 41.3 %psum.114 = f32[32]{0:T(128)S(1)} all-reduce(f32[32]{0:T(128)S(1)} %multiply_reduce_fusion.12), channel_id=1, replica_groups=mesh['sx'=8,'sy'=4] {'sx','sy'}, use_global_device_ids=true, to_apply=%region_17.21 | all-reduce | flops 32 | bytes 256 | tf_op jit(solution)/shard_map/psum | solution.py:78
  120.1 4.6 collective-permute-start.11
  127.3 39.4 %psum.115 = f32[32]{0:T(128)S(1)} all-reduce(f32[32]{0:T(128)S(1)} %get-tuple-element.109), channel_id=1, replica_groups=mesh['sx'=8,'sy'=4] {'sx','sy'}, use_global_device_ids=true, to_apply=%region_19.23 | all-reduce | flops 32 | bytes 256 | tf_op jit(solution)/shard_map/psum | solution.py:89
  166.7 40.3 %psum.116 = f32[32]{0:T(128)S(1)} all-reduce(f32[32]{0:T(128)S(1)} %get-tuple-element.74), channel_id=1, replica_groups=mesh['sx'=8,'sy'=4] {'sx','sy'}, use_global_device_ids=true, to_apply=%region_21.25 | all-reduce | flops 32 | bytes 256 | tf_op jit(solution)/shard_map/psum | solution.py:78
  210.4 3.8 collective-permute-start.13
  219.0 4.0 collective-permute-start.15
  225.6 40.9 %psum.117 = f32[32]{0:T(128)S(1)} all-reduce(f32[32]{0:T(128)S(1)} %get-tuple-element.111), channel_id=1, replica_groups=mesh['sx'=8,'sy'=4] {'sx','sy'}, use_global_device_ids=true, to_apply=%region_23.27 | all-reduce | flops 32 | bytes 256 | tf_op jit(solution)/shard_map/psum | solution.py:89
  266.5 41.2 %psum.118 = f32[32]{0:T(128)S(1)} all-reduce(f32[32]{0:T(128)S(1)} %get-tuple-element.72), channel_id=1, replica_groups=mesh['sx'=8,'sy'=4] {'sx','sy'}, use_global_device_ids=true, to_apply=%region_25.29 | all-reduce | flops 32 | bytes 256 | tf_op jit(solution)/shard_map/psum | solution.py:78
  311.1 3.8 collective-permute-start.17
  322.2 4.0 collective-permute-start.19
  327.5 41.1 %psum.119 = f32[32]{0:T(128)S(1)} all-reduce(f32[32]{0:T(128)S(1)} %get-tuple-element.113), channel_id=1, replica_groups=mesh['sx'=8,'sy'=4] {'sx','sy'}, use_global_device_ids=true, to_apply=%region_27.31 | all-reduce | flops 32 | bytes 256 | tf_op jit(solution)/shard_map/psum | solution.py:89
  368.6 40.1 %psum.120 = f32[32]{0:T(128)S(1)} all-reduce(f32[32]{0:T(128)S(1)} %get-tuple-element.70), channel_id=1, replica_groups=mesh['sx'=8,'sy'=4] {'sx','sy'}, use_global_device_ids=true, to_apply=%region_29.33 | all-reduce | flops 32 | bytes 256 | tf_op jit(solution)/shard_map/psum | solution.py:78
  412.3 3.8 collective-permute-start.21
  420.5 4.0 collective-permute-start.23
  425.7 39.1 %psum.121 = f32[32]{0:T(128)S(1)} all-reduce(f32[32]{0:T(128)S(1)} %get-tuple-element.115), channel_id=1, replica_groups=mesh['sx'=8,'sy'=4] {'sx','sy'}, use_global_device_ids=true, to_apply=%region_31.35 | all-reduce | flops 32 | bytes 256 | tf_op jit(solution)/shard_map/psum | solution.py:89
  464.8 40.4 %psum.122 = f32[32]{0:T(128)S(1)} all-reduce(f32[32]{0:T(128)S(1)} %get-tuple-element.68), channel_id=1, replica_groups=mesh['sx'=8,'sy'=4] {'sx','sy'}, use_global_device_ids=true, to_apply=%region_33.37 | all-reduce | flops 32 | bytes 256 | tf_op jit(solution)/shard_map/psum | solution.py:78
  508.7 3.8 collective-permute-start.25
  515.7 4.0 collective-permute-start.27
  520.9 52.7 %psum.123 = f32[32]{0:T(128)S(1)} all-reduce(f32[32]{0:T(128)S(1)} %get-tuple-element.117), channel_id=1, replica_groups=mesh['sx'=8,'sy'=4] {'sx','sy'}, use_global_device_ids=true, to_apply=%region_35.39 | all-reduce | flops 32 | bytes 256 | tf_op jit(solution)/shard_map/psum | solution.py:89
  573.6 41.2 %psum.124 = f32[32]{0:T(128)S(1)} all-reduce(f32[32]{0:T(128)S(1)} %get-tuple-element.66), channel_id=1, replica_groups=mesh['sx'=8,'sy'=4] {'sx','sy'}, use_global_device_ids=true, to_apply=%region_37.41 | all-reduce | flops 32 | bytes 256 | tf_op jit(solution)/shard_map/psum | solution.py:78
  618.3 3.8 collective-permute-start.29
  625.7 4.0 collective-permute-start.31
  631.6 39.8 %psum.125 = f32[32]{0:T(128)S(1)} all-reduce(f32[32]{0:T(128)S(1)} %get-tuple-element.119), channel_id=1, replica_groups=mesh['sx'=8,'sy'=4] {'sx','sy'}, use_global_device_ids=true, to_apply=%region_39.43 | all-reduce | flops 32 | bytes 256 | tf_op jit(solution)/shard_map/psum | solution.py:89
  671.9 40.3 %psum.126 = f32[32]{0:T(128)S(1)} all-reduce(f32[32]{0:T(128)S(1)} %multiply_reduce_fusion), channel_id=1, replica_groups=mesh['sx'=8,'sy'=4] {'sx','sy'}, use_global_device_ids=true, to_apply=%region_41.45 | all-reduce | flops 32 | bytes 256 | tf_op jit(solution)/shard_map/psum | solution.py:78
  726.0 23.5 %collective-permute-done.36 = f32[3,1,6,32]{3,2,1,0:T(8,128)S(1)} collective-permute-done((f32[3,1,6,32]{3,2,1,0:T(8,128)S(1)}, f32[3,1,6,32]{3,2,1,0:T(8,128)S(1)}, u32[]{:S(2)}, u32[]{:S(2)}) %collective-permute-start.36) | collective-permute-done | bytes 2336 | tf_op jit(solution)/shard_map/ppermute | solution.py:26
  755.8 39.7 %psum.127 = f32[32]{0:T(128)S(1)} all-reduce(f32[32]{0:T(128)S(1)} %fusion.26), channel_id=1, replica_groups=mesh['sx'=8,'sy'=4] {'sx','sy'}, use_global_device_ids=true, to_apply=%region_43.47 | all-reduce | flops 32 | bytes 256 | tf_op jit(solution)/shard_map/psum | solution.py:89
  799.2 11.7 %cholesky.286 = f32[128,128]{1,0:T(8,128)S(1)} custom-call(f32[128,128]{1,0:T(8,128)S(1)} %cholesky.426), custom_call_target="Cholesky" | custom-call | tf_op jit(solution)/shard_map/jit(cholesky)/cholesky | solution.py:35
  810.9 9.8 custom-call.31
  823.4 11.7 %cholesky.305 = f32[128,128]{1,0:T(8,128)S(1)} custom-call(f32[128,128]{1,0:T(8,128)S(1)} %cholesky.430), custom_call_target="Cholesky" | custom-call | tf_op jit(solution)/shard_map/jit(cholesky)/cholesky | solution.py:35
  835.2 10.2 custom-call.32
  846.9 11.7 %cholesky.326 = f32[128,128]{1,0:T(8,128)S(1)} custom-call(f32[128,128]{1,0:T(8,128)S(1)} %cholesky.435), custom_call_target="Cholesky" | custom-call | tf_op jit(solution)/shard_map/jit(cholesky)/cholesky | solution.py:35
  859.4 9.8 custom-call.33
  870.6 11.9 %cholesky.343 = f32[128,128]{1,0:T(8,128)S(1)} custom-call(f32[128,128]{1,0:T(8,128)S(1)} %slice_subtract_fusion.5), custom_call_target="Cholesky" | custom-call | tf_op jit(solution)/shard_map/jit(cholesky)/cholesky | solution.py:35
  887.3 10.3 while.8
  897.5 40.7 %custom-call.35 = f32[4,128,128]{1,2,0:T(8,128)} custom-call(f32[4,128,128]{2,1,0:T(8,128)} %get-tuple-element.35), custom_call_target="InvertDiagBlocksLowerTriangular" | custom-call | tf_op jit(solution)/shard_map/jit(_solve_triangular)/triangular_solve | solution.py:38
  946.1 5.3 collective-permute-start.2
  953.5 11.7 %cholesky.358 = f32[128,128]{1,0:T(8,128)S(1)} custom-call(f32[128,128]{1,0:T(8,128)S(1)} %cholesky.439), custom_call_target="Cholesky" | custom-call | tf_op jit(solution)/shard_map/jit(cholesky)/cholesky | solution.py:35
  965.2 9.8 custom-call.36
  975.8 11.7 %cholesky.377 = f32[128,128]{1,0:T(8,128)S(1)} custom-call(f32[128,128]{1,0:T(8,128)S(1)} %cholesky.443), custom_call_target="Cholesky" | custom-call | tf_op jit(solution)/shard_map/jit(cholesky)/cholesky | solution.py:35
  987.6 10.0 custom-call.37
  998.3 11.7 %cholesky.398 = f32[128,128]{1,0:T(8,128)S(1)} custom-call(f32[128,128]{1,0:T(8,128)S(1)} %cholesky.448), custom_call_target="Cholesky" | custom-call | tf_op jit(solution)/shard_map/jit(cholesky)/cholesky | solution.py:35
  1010.6 9.8 custom-call.38
  1021.1 11.7 %cholesky.415 = f32[128,128]{1,0:T(8,128)S(1)} custom-call(f32[128,128]{1,0:T(8,128)S(1)} %slice_subtract_fusion.4), custom_call_target="Cholesky" | custom-call | tf_op jit(solution)/shard_map/jit(cholesky)/cholesky | solution.py:35
  1037.2 8.2 while.9
  1045.4 39.3 %custom-call.40 = f32[4,128,128]{1,2,0:T(8,128)S(1)} custom-call(f32[4,128,128]{2,1,0:T(8,128)S(1)} %get-tuple-element.37), custom_call_target="InvertDiagBlocksLowerTriangular" | custom-call | tf_op jit(solution)/shard_map/jit(_solve_triangular)/triangular_solve | solution.py:38
  (303 shorter events, 154.4 us)
Async XLA Ops:
  3.7 14.8 %collective-permute-start.6 = (f32[1,1,6,32]{3,2,1,0:T(8,128)S(1)}, f32[1,1,6,32]{3,2,1,0:T(8,128)S(1)}, u32[]{:S(2)}, u32[]{:S(2)}) collective-permute-start(f32[1,1,6,32]{3,2,1,0:T(8,128)S(1)} %bitcast.395), channel_id=1, source_target_pairs={{4,0},{8,4},{12,8},{16,12},{20,16},{24,20},{28,24},{5,1},{9,5},{13... | collective-permute-start | bytes 2312 | tf_op jit(solution)/shard_map/ppermute | solution.py:26
  5.6 12.9 %collective-permute-start.5 = (f32[1,1,6,32]{3,2,1,0:T(8,128)S(1)}, f32[1,1,6,32]{3,2,1,0:T(8,128)S(1)}, u32[]{:S(2)}, u32[]{:S(2)}) collective-permute-start(f32[1,1,6,32]{3,2,1,0:T(8,128)S(1)} %bitcast.396), channel_id=1, source_target_pairs={{0,4},{4,8},{8,12},{12,16},{16,20},{20,24},{24,28},{1,5},{5,9},{9,... | collective-permute-start | bytes 2312 | tf_op jit(solution)/shard_map/ppermute | solution.py:24
  10.8 4.6 collective-permute-start.4
  12.8 4.9 collective-permute-start.3
  18.5 502.2 %copy-start.18 = (f32[6]{0:T(128)}, f32[6]{0:T(128)S(1)}, u32[]{:S(2)}) copy-start(f32[6]{0:T(128)S(1)} %bitcast_add_fusion.4) | copy-start | bytes 76
  18.5 6.1 collective-permute-start.8
  19.8 5.4 collective-permute-start.7
  108.8 10.0 collective-permute-start.10
  112.2 6.6 collective-permute-start.9
  117.5 967.2 %collective-permute-start.38 = (f32[32,512]{1,0:T(8,128)}, f32[32,512]{1,0:T(8,128)}, u32[]{:S(2)}, u32[]{:S(2)}) collective-permute-start(f32[32,512]{1,0:T(8,128)} %slice_bitcast_fusion.8), channel_id=1, source_target_pairs={{1,0},{2,1},{3,2},{5,4},{6,5},{7,6},{9,8},{10,9},{11,10},{13,12},{... | collective-permute-start | bytes 196616 | tf_op jit(solution)/shard_map/ppermute | solution.py:13
  118.8 6.1 collective-permute-start.12
  120.1 5.4 collective-permute-start.11
  166.7 52.3 %copy-start.13 = (f32[32]{0:T(128)}, f32[32]{0:T(128)S(1)}, u32[]{:S(2)}) copy-start(f32[32]{0:T(128)S(1)} %div.53) | copy-start | bytes 388
  207.1 10.6 collective-permute-start.14
  210.4 7.2 collective-permute-start.13
  215.7 722.5 %collective-permute-start.1 = (f32[32,512]{1,0:T(8,128)}, f32[32,512]{1,0:T(8,128)}, u32[]{:S(2)}, u32[]{:S(2)}) collective-permute-start(f32[32,512]{1,0:T(8,128)} %slice_bitcast_fusion.9), channel_id=1, source_target_pairs={{4,0},{8,4},{12,8},{16,12},{20,16},{24,20},{28,24},{5,1},{9,5},{13... | collective-permute-start | bytes 196616 | tf_op jit(solution)/shard_map/ppermute | solution.py:13
  217.7 5.4 collective-permute-start.16
  219.0 4.8 collective-permute-start.15
  307.7 13.2 %collective-permute-start.18 = (f32[1,1,6,32]{3,2,1,0:T(8,128)S(1)}, f32[1,1,6,32]{3,2,1,0:T(8,128)S(1)}, u32[]{:S(2)}, u32[]{:S(2)}) collective-permute-start(f32[1,1,6,32]{3,2,1,0:T(8,128)S(1)} %bitcast.402), channel_id=1, source_target_pairs={{4,0},{8,4},{12,8},{16,12},{20,16},{24,20},{28,24},{5,1},{9,5},{13... | collective-permute-start | bytes 2312 | tf_op jit(solution)/shard_map/ppermute | solution.py:26
  311.1 9.8 collective-permute-start.17
  319.0 478.4 %collective-permute-start = (f32[512,512]{0,1:T(8,128)}, f32[512,512]{0,1:T(8,128)S(1)}, u32[]{:S(2)}, u32[]{:S(2)}) collective-permute-start(f32[512,512]{0,1:T(8,128)} %bitcast.3), channel_id=1, source_target_pairs={{4,0},{8,4},{12,8},{16,12},{20,16},{24,20},{28,24},{5,1},{9,5},{13... | collective-permute-start | bytes 3145736 | tf_op jit(solution)/shard_map/ppermute | solution.py:13
  320.9 5.4 collective-permute-start.20
  322.2 4.8 collective-permute-start.19
  408.7 103.7 %copy-start = (f32[2,1,512,512]{3,2,1,0:T(8,128)S(1)}, f32[2,1,512,512]{3,2,1,0:T(8,128)}, u32[]{:S(2)}) copy-start(f32[2,1,512,512]{3,2,1,0:T(8,128)} %param.14) | copy-start | bytes 6291460
  408.7 103.7 %copy-start.5 = (f32[2,1,32,512]{3,2,1,0:T(8,128)S(1)}, f32[2,1,32,512]{3,2,1,0:T(8,128)}, u32[]{:S(2)}) copy-start(f32[2,1,32,512]{3,2,1,0:T(8,128)} %param.16) | copy-start | bytes 393220
  408.8 213.3 %copy-start.6 = (f32[1,2,32,512]{3,2,1,0:T(8,128)S(1)}, f32[1,2,32,512]{3,2,1,0:T(8,128)}, u32[]{:S(2)}) copy-start(f32[1,2,32,512]{3,2,1,0:T(8,128)} %param.17) | copy-start | bytes 393220
  408.8 10.4 collective-permute-start.22
  412.3 6.9 collective-permute-start.21
  419.2 5.4 collective-permute-start.24
  420.5 4.8 collective-permute-start.23
  505.3 8.9 collective-permute-start.26
  508.7 5.5 collective-permute-start.25
  514.2 205.4 %copy-start.2 = (f32[1,1,512,512]{3,2,1,0:T(8,128)S(1)}, f32[1,1,512,512]{3,2,1,0:T(8,128)}, u32[]{:S(2)}) copy-start(f32[1,1,512,512]{3,2,1,0:T(8,128)} %get-tuple-element.84) | copy-start | bytes 3145732
  514.2 5.6 collective-permute-start.28
  515.7 4.8 collective-permute-start.27
  614.9 9.5 collective-permute-start.30
  618.3 6.1 collective-permute-start.29
  624.4 5.4 collective-permute-start.32
  625.7 4.8 collective-permute-start.31
  712.3 10.3 collective-permute-start.34
  715.7 8.2 collective-permute-start.33
  722.6 228.8 %collective-permute-start.37 = (f32[512,512]{0,1:T(8,128)}, f32[512,512]{0,1:T(8,128)}, u32[]{:S(2)}, u32[]{:S(2)}) collective-permute-start(f32[512,512]{0,1:T(8,128)} %bitcast.390), channel_id=1, source_target_pairs={{1,0},{2,1},{3,2},{5,4},{6,5},{7,6},{9,8},{10,9},{11,10},{13,12},{... | collective-permute-start | bytes 3145736 | tf_op jit(solution)/shard_map/ppermute | solution.py:13
  724.6 24.9 %collective-permute-start.36 = (f32[3,1,6,32]{3,2,1,0:T(8,128)S(1)}, f32[3,1,6,32]{3,2,1,0:T(8,128)S(1)}, u32[]{:S(2)}, u32[]{:S(2)}) collective-permute-start(f32[3,1,6,32]{3,2,1,0:T(8,128)S(1)} %pad_maximum_fusion.7), channel_id=1, source_target_pairs={{1,0},{2,1},{3,2},{5,4},{6,5},{7,6},{9,8},{10,9},{11,10},{13,12},{... | collective-permute-start | bytes 6920 | tf_op jit(solution)/shard_map/ppermute | solution.py:26
  749.5 3.9 collective-permute-start.35
  887.3 64.2 %copy-start.1 = (f32[1,1,512,512]{2,3,1,0:T(8,128)S(1)}, f32[1,1,512,512]{2,3,1,0:T(8,128)}, u32[]{:S(2)}) copy-start(f32[1,1,512,512]{2,3,1,0:T(8,128)} %copy.41) | copy-start | bytes 3145732
  946.1 145.2 %collective-permute-start.2 = (f32[32,512]{1,0:T(8,128)}, f32[32,512]{1,0:T(8,128)}, u32[]{:S(2)}, u32[]{:S(2)}) collective-permute-start(f32[32,512]{1,0:T(8,128)} %get-tuple-element.77), channel_id=1, source_target_pairs={{0,4},{4,8},{8,12},{12,16},{16,20},{20,24},{24,28},{1,5},{5,9},{9,... | collective-permute-start | bytes 196616 | tf_op jit(solution)/shard_map/ppermute | solution.py:13
  1037.1 55.1 %copy-start.9 = (f32[1,32,512]{2,1,0:T(8,128)S(1)}, f32[1,32,512]{2,1,0:T(8,128)}, u32[]{:S(2)}) copy-start(f32[1,32,512]{2,1,0:T(8,128)} %get-tuple-element.76) | copy-start | bytes 196612
  1089.7 3.5 collective-permute-start.39
  (13 other events, 384.3 us)
where the time goes:
time: 1110 us; the launch traced here: 1090 us
  blocking collectives  618 us (56%)
  other arithmetic  248 us (22%)
  starting transfers between devices  116 us (10%)
  matrix products  38.3 us (3%)
  local copies, waits for them, and re-layouts  36.8 us (3%)
  waiting for transfers between devices  30.2 us (3%)
    psum x8, blocking collectives, squares(): return lax.psum(jnp.sum(values * values, axis=0), ('sx', 'sy'))  325 us
    psum x7, blocking collectives, shards(): curve = lax.psum(jnp.sum(direction * image, axis=0), ('sx', 'sy'))  293 us
    another operation x28, other arithmetic, face_average(): factor = jnp.linalg.cholesky(summed)  158 us
    another operation x5, other arithmetic, face_average(): jax.scipy.linalg.solve_triangular(factor, forward, lower=True, trans=1)  80.8 us
    ppermute x16, starting transfers between devices, with_halo(): lax.ppermute(tail, axis, [(i, (i + 1) % count) for i in range(ends)])  63.3 us
    ppermute x16, starting transfers between devices, with_halo(): lax.ppermute(head, axis, [((i + 1) % count, i) for i in range(ends)])  36.3 us
    ppermute x16, waiting for transfers between devices, with_halo(): lax.ppermute(head, axis, [((i + 1) % count, i) for i in range(ends)])  23.5 us
  transfers between devices with their start and end apart: 40, of which 10 were waited for; matrix products, arithmetic and copies ran while one was open for 29% of the time, Pallas kernels for 0%

commit v1 on v0

--- a/solution.py
+++ b/solution.py
@@ -86,7 +86,9 @@
         image = image + jnp.dot(next_x, padded[2, 1], precision=HIGH)
         image = image + jnp.dot(link_y.T, padded[1, 0], precision=HIGH)
         image = image + jnp.dot(next_y, padded[1, 2], precision=HIGH)
-        curve = lax.psum(jnp.sum(direction * image, axis=0), ("sx", "sy"))
+        curve = jnp.sum(direction * image, axis=0)
+        for name in ("sy", "sx"):
+            curve = lax.psum(curve, name)
         alpha = norm_now / curve
         coarse = coarse + alpha * direction
         remain = remain - alpha * image

time: 1110 us -> 988 us (0.89)
  blocking collectives: 618 us -> 499 us
    psum x7 -> x16, blocking collectives: 293 us -> 195 us  [shards(): curve = lax.psum(curve, name)]
    psum x8, blocking collectives: 325 us -> 304 us  [squares(): return lax.psum(jnp.sum(values * values, axis=0), ('sx', 'sy'))]
  transfers between devices with their start and end apart: 40 -> 40, of which waited for: 10 -> 10; matrix products, arithmetic and copies ran while one was open for 29% -> 32% of each run, Pallas kernels for 0% -> 0%
where the time goes in v1:
time: 988 us; the launch traced here: 975 us
  blocking collectives  499 us (51%)
  other arithmetic  248 us (25%)
  starting transfers between devices  116 us (12%)
  matrix products  37.6 us (4%)
  local copies, waits for them, and re-layouts  36.8 us (4%)
  waiting for transfers between devices  29.2 us (3%)
    psum x8, blocking collectives, squares(): return lax.psum(jnp.sum(values * values, axis=0), ('sx', 'sy'))  304 us
    psum x16, blocking collectives, shards(): curve = lax.psum(curve, name)  195 us
    another operation x28, other arithmetic, face_average(): factor = jnp.linalg.cholesky(summed)  158 us
    another operation x5, other arithmetic, face_average(): jax.scipy.linalg.solve_triangular(factor, forward, lower=True, trans=1)  80.8 us
    ppermute x16, starting transfers between devices, with_halo(): lax.ppermute(tail, axis, [(i, (i + 1) % count) for i in range(ends)])  67.3 us
    ppermute x16, starting transfers between devices, with_halo(): lax.ppermute(head, axis, [((i + 1) % count, i) for i in range(ends)])  36.1 us
    ppermute x16, waiting for transfers between devices, with_halo(): lax.ppermute(head, axis, [((i + 1) % count, i) for i in range(ends)])  23.9 us
  transfers between devices with their start and end apart: 40, of which 10 were waited for; matrix products, arithmetic and copies ran while one was open for 32% of the time, Pallas kernels for 0%

profile of v1, /device:TPU:1, one launch (start us, length us, event | category | flops | bytes accessed | tf_op | source)
XLA Modules:
  0.0 974.6 jit_solution(10541210328815648130)
XLA Ops:
  27.0 10.5 %psum.169 = f32[32]{0:T(128)S(1)} all-reduce(f32[32]{0:T(128)S(1)} %get-tuple-element.44), channel_id=1, replica_groups=mesh['sx'=8,'sy'=4] {'sy'}, use_global_device_ids=true, to_apply=%region_15.19 | all-reduce | flops 32 | bytes 256 | tf_op jit(solution)/shard_map/psum | solution.py:91
  37.5 14.5 %psum.170 = f32[32]{0:T(128)S(1)} all-reduce(f32[32]{0:T(128)S(1)} %psum.169), channel_id=1, replica_groups=mesh['sx'=8,'sy'=4] {'sx'}, use_global_device_ids=true, to_apply=%region_16.20 | all-reduce | flops 32 | bytes 256 | tf_op jit(solution)/shard_map/psum | solution.py:91
  52.0 37.5 %psum.168 = f32[32]{0:T(128)S(1)} all-reduce(f32[32]{0:T(128)S(1)} %get-tuple-element.45), channel_id=1, replica_groups=mesh['sx'=8,'sy'=4] {'sx','sy'}, use_global_device_ids=true, to_apply=%region_9.13 | all-reduce | flops 32 | bytes 256 | tf_op jit(solution)/shard_map/psum | solution.py:78
  90.8 44.0 %psum.171 = f32[32]{0:T(128)S(1)} all-reduce(f32[32]{0:T(128)S(1)} %multiply_reduce_fusion.12), channel_id=1, replica_groups=mesh['sx'=8,'sy'=4] {'sx','sy'}, use_global_device_ids=true, to_apply=%region_18.22 | all-reduce | flops 32 | bytes 256 | tf_op jit(solution)/shard_map/psum | solution.py:78
  153.3 10.0 %psum.172 = f32[32]{0:T(128)S(1)} all-reduce(f32[32]{0:T(128)S(1)} %get-tuple-element.107), channel_id=1, replica_groups=mesh['sx'=8,'sy'=4] {'sy'}, use_global_device_ids=true, to_apply=%region_20.24 | all-reduce | flops 32 | bytes 256 | tf_op jit(solution)/shard_map/psum | solution.py:91
  163.3 13.8 %psum.173 = f32[32]{0:T(128)S(1)} all-reduce(f32[32]{0:T(128)S(1)} %psum.172), channel_id=1, replica_groups=mesh['sx'=8,'sy'=4] {'sx'}, use_global_device_ids=true, to_apply=%region_21.25 | all-reduce | flops 32 | bytes 256 | tf_op jit(solution)/shard_map/psum | solution.py:91
  177.2 37.7 %psum.174 = f32[32]{0:T(128)S(1)} all-reduce(f32[32]{0:T(128)S(1)} %get-tuple-element.72), channel_id=1, replica_groups=mesh['sx'=8,'sy'=4] {'sx','sy'}, use_global_device_ids=true, to_apply=%region_23.27 | all-reduce | flops 32 | bytes 256 | tf_op jit(solution)/shard_map/psum | solution.py:78
  229.3 5.1 collective-permute-start.15
  235.6 9.8 %psum.175 = f32[32]{0:T(128)S(1)} all-reduce(f32[32]{0:T(128)S(1)} %get-tuple-element.109), channel_id=1, replica_groups=mesh['sx'=8,'sy'=4] {'sy'}, use_global_device_ids=true, to_apply=%region_25.29 | all-reduce | flops 32 | bytes 256 | tf_op jit(solution)/shard_map/psum | solution.py:91
  245.5 15.4 %psum.176 = f32[32]{0:T(128)S(1)} all-reduce(f32[32]{0:T(128)S(1)} %psum.175), channel_id=1, replica_groups=mesh['sx'=8,'sy'=4] {'sx'}, use_global_device_ids=true, to_apply=%region_26.30 | all-reduce | flops 32 | bytes 256 | tf_op jit(solution)/shard_map/psum | solution.py:91
  260.9 37.1 %psum.177 = f32[32]{0:T(128)S(1)} all-reduce(f32[32]{0:T(128)S(1)} %get-tuple-element.70), channel_id=1, replica_groups=mesh['sx'=8,'sy'=4] {'sx','sy'}, use_global_device_ids=true, to_apply=%region_28.32 | all-reduce | flops 32 | bytes 256 | tf_op jit(solution)/shard_map/psum | solution.py:78
  309.7 4.7 collective-permute-start.19
  315.6 9.7 psum.178
  325.3 14.3 %psum.179 = f32[32]{0:T(128)S(1)} all-reduce(f32[32]{0:T(128)S(1)} %psum.178), channel_id=1, replica_groups=mesh['sx'=8,'sy'=4] {'sx'}, use_global_device_ids=true, to_apply=%region_31.35 | all-reduce | flops 32 | bytes 256 | tf_op jit(solution)/shard_map/psum | solution.py:91
  339.6 36.5 %psum.180 = f32[32]{0:T(128)S(1)} all-reduce(f32[32]{0:T(128)S(1)} %get-tuple-element.68), channel_id=1, replica_groups=mesh['sx'=8,'sy'=4] {'sx','sy'}, use_global_device_ids=true, to_apply=%region_33.37 | all-reduce | flops 32 | bytes 256 | tf_op jit(solution)/shard_map/psum | solution.py:78
  386.5 4.7 collective-permute-start.23
  392.4 9.7 psum.181
  402.1 14.9 %psum.182 = f32[32]{0:T(128)S(1)} all-reduce(f32[32]{0:T(128)S(1)} %psum.181), channel_id=1, replica_groups=mesh['sx'=8,'sy'=4] {'sx'}, use_global_device_ids=true, to_apply=%region_36.40 | all-reduce | flops 32 | bytes 256 | tf_op jit(solution)/shard_map/psum | solution.py:91
  417.1 37.1 %psum.183 = f32[32]{0:T(128)S(1)} all-reduce(f32[32]{0:T(128)S(1)} %get-tuple-element.66), channel_id=1, replica_groups=mesh['sx'=8,'sy'=4] {'sx','sy'}, use_global_device_ids=true, to_apply=%region_38.42 | all-reduce | flops 32 | bytes 256 | tf_op jit(solution)/shard_map/psum | solution.py:78
  465.0 4.7 collective-permute-start.27
  471.6 9.7 psum.184
  481.3 14.5 %psum.185 = f32[32]{0:T(128)S(1)} all-reduce(f32[32]{0:T(128)S(1)} %psum.184), channel_id=1, replica_groups=mesh['sx'=8,'sy'=4] {'sx'}, use_global_device_ids=true, to_apply=%region_41.45 | all-reduce | flops 32 | bytes 256 | tf_op jit(solution)/shard_map/psum | solution.py:91
  495.8 37.1 %psum.186 = f32[32]{0:T(128)S(1)} all-reduce(f32[32]{0:T(128)S(1)} %get-tuple-element.64), channel_id=1, replica_groups=mesh['sx'=8,'sy'=4] {'sx','sy'}, use_global_device_ids=true, to_apply=%region_43.47 | all-reduce | flops 32 | bytes 256 | tf_op jit(solution)/shard_map/psum | solution.py:78
  542.1 4.7 collective-permute-start.31
  548.7 9.7 psum.187
  558.3 16.1 %psum.188 = f32[32]{0:T(128)S(1)} all-reduce(f32[32]{0:T(128)S(1)} %psum.187), channel_id=1, replica_groups=mesh['sx'=8,'sy'=4] {'sx'}, use_global_device_ids=true, to_apply=%region_46.50 | all-reduce | flops 32 | bytes 256 | tf_op jit(solution)/shard_map/psum | solution.py:91
  574.4 37.1 %psum.189 = f32[32]{0:T(128)S(1)} all-reduce(f32[32]{0:T(128)S(1)} %multiply_reduce_fusion), channel_id=1, replica_groups=mesh['sx'=8,'sy'=4] {'sx','sy'}, use_global_device_ids=true, to_apply=%region_48.52 | all-reduce | flops 32 | bytes 256 | tf_op jit(solution)/shard_map/psum | solution.py:78
  626.5 23.9 %collective-permute-done.36 = f32[3,1,6,32]{3,2,1,0:T(8,128)S(1)} collective-permute-done((f32[3,1,6,32]{3,2,1,0:T(8,128)S(1)}, f32[3,1,6,32]{3,2,1,0:T(8,128)S(1)}, u32[]{:S(2)}, u32[]{:S(2)}) %collective-permute-start.36) | collective-permute-done | bytes 2336 | tf_op jit(solution)/shard_map/ppermute | solution.py:26
  656.0 8.3 psum.190
  664.3 14.6 %psum.191 = f32[32]{0:T(128)S(1)} all-reduce(f32[32]{0:T(128)S(1)} %psum.190), channel_id=1, replica_groups=mesh['sx'=8,'sy'=4] {'sx'}, use_global_device_ids=true, to_apply=%region_51.55 | all-reduce | flops 32 | bytes 256 | tf_op jit(solution)/shard_map/psum | solution.py:91
  682.7 11.7 %cholesky.286 = f32[128,128]{1,0:T(8,128)S(1)} custom-call(f32[128,128]{1,0:T(8,128)S(1)} %cholesky.426), custom_call_target="Cholesky" | custom-call | tf_op jit(solution)/shard_map/jit(cholesky)/cholesky | solution.py:35
  694.4 9.8 %custom-call.31 = f32[1,128,128]{1,2,0:T(8,128)S(1)} custom-call(f32[1,128,128]{2,1,0:T(8,128)S(1)} %get-tuple-element.103), custom_call_target="InvertDiagBlocksLowerTriangular" | custom-call | tf_op jit(solution)/shard_map/jit(cholesky)/cholesky | solution.py:35
  706.9 11.7 %cholesky.305 = f32[128,128]{1,0:T(8,128)S(1)} custom-call(f32[128,128]{1,0:T(8,128)S(1)} %cholesky.430), custom_call_target="Cholesky" | custom-call | tf_op jit(solution)/shard_map/jit(cholesky)/cholesky | solution.py:35
  718.6 10.2 %custom-call.32 = f32[1,128,128]{1,2,0:T(8,128)S(1)} custom-call(f32[1,128,128]{2,1,0:T(8,128)S(1)} %get-tuple-element.100), custom_call_target="InvertDiagBlocksLowerTriangular" | custom-call | tf_op jit(solution)/shard_map/jit(cholesky)/cholesky | solution.py:35
  730.4 11.7 %cholesky.326 = f32[128,128]{1,0:T(8,128)S(1)} custom-call(f32[128,128]{1,0:T(8,128)S(1)} %cholesky.435), custom_call_target="Cholesky" | custom-call | tf_op jit(solution)/shard_map/jit(cholesky)/cholesky | solution.py:35
  742.8 9.8 %custom-call.33 = f32[1,128,128]{1,2,0:T(8,128)S(1)} custom-call(f32[1,128,128]{2,1,0:T(8,128)S(1)} %get-tuple-element.97), custom_call_target="InvertDiagBlocksLowerTriangular" | custom-call | tf_op jit(solution)/shard_map/jit(cholesky)/cholesky | solution.py:35
  754.1 11.9 %cholesky.343 = f32[128,128]{1,0:T(8,128)S(1)} custom-call(f32[128,128]{1,0:T(8,128)S(1)} %slice_subtract_fusion.5), custom_call_target="Cholesky" | custom-call | tf_op jit(solution)/shard_map/jit(cholesky)/cholesky | solution.py:35
  770.7 10.3 %while.8 = (s32[]{:T(128)}, f32[512,512]{1,0:T(8,128)S(1)}, s32[4,2]{0,1:T(2,128)S(1)}, f32[4,128,128]{2,1,0:T(8,128)}, s32[]{:T(128)}) while((s32[]{:T(128)}, f32[512,512]{1,0:T(8,128)S(1)}, s32[4,2]{0,1:T(2,128)S(1)}, f32[4,128,128]{2,1,0:T(8,128)}, s32[]{:T(128)}) %tuple.84), condition=%wide.while_cond.1, body=%wide.while_body.1.sunk | while | flops 2 | bytes 132205 | solution.py:38
  781.0 40.7 %custom-call.35 = f32[4,128,128]{1,2,0:T(8,128)} custom-call(f32[4,128,128]{2,1,0:T(8,128)} %get-tuple-element.35), custom_call_target="InvertDiagBlocksLowerTriangular" | custom-call | tf_op jit(solution)/shard_map/jit(_solve_triangular)/triangular_solve | solution.py:38
  833.6 11.7 %cholesky.358 = f32[128,128]{1,0:T(8,128)S(1)} custom-call(f32[128,128]{1,0:T(8,128)S(1)} %cholesky.439), custom_call_target="Cholesky" | custom-call | tf_op jit(solution)/shard_map/jit(cholesky)/cholesky | solution.py:35
  845.3 9.8 %custom-call.36 = f32[1,128,128]{1,2,0:T(8,128)S(1)} custom-call(f32[1,128,128]{2,1,0:T(8,128)S(1)} %get-tuple-element.93), custom_call_target="InvertDiagBlocksLowerTriangular" | custom-call | tf_op jit(solution)/shard_map/jit(cholesky)/cholesky | solution.py:35
  855.9 11.7 %cholesky.377 = f32[128,128]{1,0:T(8,128)S(1)} custom-call(f32[128,128]{1,0:T(8,128)S(1)} %cholesky.443), custom_call_target="Cholesky" | custom-call | tf_op jit(solution)/shard_map/jit(cholesky)/cholesky | solution.py:35
  867.7 10.0 %custom-call.37 = f32[1,128,128]{1,2,0:T(8,128)S(1)} custom-call(f32[1,128,128]{2,1,0:T(8,128)S(1)} %get-tuple-element.90), custom_call_target="InvertDiagBlocksLowerTriangular" | custom-call | tf_op jit(solution)/shard_map/jit(cholesky)/cholesky | solution.py:35
  878.4 11.7 %cholesky.398 = f32[128,128]{1,0:T(8,128)S(1)} custom-call(f32[128,128]{1,0:T(8,128)S(1)} %cholesky.448), custom_call_target="Cholesky" | custom-call | tf_op jit(solution)/shard_map/jit(cholesky)/cholesky | solution.py:35
  890.8 9.8 %custom-call.38 = f32[1,128,128]{1,2,0:T(8,128)S(1)} custom-call(f32[1,128,128]{2,1,0:T(8,128)S(1)} %get-tuple-element.87), custom_call_target="InvertDiagBlocksLowerTriangular" | custom-call | tf_op jit(solution)/shard_map/jit(cholesky)/cholesky | solution.py:35
  901.2 11.7 %cholesky.415 = f32[128,128]{1,0:T(8,128)S(1)} custom-call(f32[128,128]{1,0:T(8,128)S(1)} %slice_subtract_fusion.4), custom_call_target="Cholesky" | custom-call | tf_op jit(solution)/shard_map/jit(cholesky)/cholesky | solution.py:35
  917.3 8.2 while.9
  925.5 39.3 %custom-call.40 = f32[4,128,128]{1,2,0:T(8,128)S(1)} custom-call(f32[4,128,128]{2,1,0:T(8,128)S(1)} %get-tuple-element.37), custom_call_target="InvertDiagBlocksLowerTriangular" | custom-call | tf_op jit(solution)/shard_map/jit(_solve_triangular)/triangular_solve | solution.py:38
  (312 shorter events, 186.7 us)
Async XLA Ops:
  3.7 14.8 %collective-permute-start.6 = (f32[1,1,6,32]{3,2,1,0:T(8,128)S(1)}, f32[1,1,6,32]{3,2,1,0:T(8,128)S(1)}, u32[]{:S(2)}, u32[]{:S(2)}) collective-permute-start(f32[1,1,6,32]{3,2,1,0:T(8,128)S(1)} %bitcast.395), channel_id=1, source_target_pairs={{4,0},{8,4},{12,8},{16,12},{20,16},{24,20},{28,24},{5,1},{9,5},{13... | collective-permute-start | bytes 2312 | tf_op jit(solution)/shard_map/ppermute | solution.py:26
  5.6 12.9 %collective-permute-start.5 = (f32[1,1,6,32]{3,2,1,0:T(8,128)S(1)}, f32[1,1,6,32]{3,2,1,0:T(8,128)S(1)}, u32[]{:S(2)}, u32[]{:S(2)}) collective-permute-start(f32[1,1,6,32]{3,2,1,0:T(8,128)S(1)} %bitcast.396), channel_id=1, source_target_pairs={{0,4},{4,8},{8,12},{12,16},{16,20},{20,24},{24,28},{1,5},{5,9},{9,... | collective-permute-start | bytes 2312 | tf_op jit(solution)/shard_map/ppermute | solution.py:24
  10.8 6.1 collective-permute-start.4
  12.8 4.9 collective-permute-start.3
  18.5 373.7 %copy-start.18 = (f32[6]{0:T(128)}, f32[6]{0:T(128)S(1)}, u32[]{:S(2)}) copy-start(f32[6]{0:T(128)S(1)} %bitcast_add_fusion.4) | copy-start | bytes 76
  18.5 6.1 collective-permute-start.8
  19.8 5.4 collective-permute-start.7
  89.5 875.3 %collective-permute-start.38 = (f32[32,512]{1,0:T(8,128)}, f32[32,512]{1,0:T(8,128)}, u32[]{:S(2)}, u32[]{:S(2)}) collective-permute-start(f32[32,512]{1,0:T(8,128)} %slice_bitcast_fusion.8), channel_id=1, source_target_pairs={{1,0},{2,1},{3,2},{5,4},{6,5},{7,6},{9,8},{10,9},{11,10},{13,12},{... | collective-permute-start | bytes 196616 | tf_op jit(solution)/shard_map/ppermute | solution.py:13
  134.8 10.6 %collective-permute-start.10 = (f32[1,1,6,32]{3,2,1,0:T(8,128)S(1)}, f32[1,1,6,32]{3,2,1,0:T(8,128)S(1)}, u32[]{:S(2)}, u32[]{:S(2)}) collective-permute-start(f32[1,1,6,32]{3,2,1,0:T(8,128)S(1)} %bitcast.414), channel_id=1, source_target_pairs={{4,0},{8,4},{12,8},{16,12},{20,16},{24,20},{28,24},{5,1},{9,5},{13... | collective-permute-start | bytes 2312 | tf_op jit(solution)/shard_map/ppermute | solution.py:26
  138.2 7.2 collective-permute-start.9
  143.5 678.3 %collective-permute-start.1 = (f32[32,512]{1,0:T(8,128)}, f32[32,512]{1,0:T(8,128)}, u32[]{:S(2)}, u32[]{:S(2)}) collective-permute-start(f32[32,512]{1,0:T(8,128)} %slice_bitcast_fusion.9), channel_id=1, source_target_pairs={{4,0},{8,4},{12,8},{16,12},{20,16},{24,20},{28,24},{5,1},{9,5},{13... | collective-permute-start | bytes 196616 | tf_op jit(solution)/shard_map/ppermute | solution.py:13
  145.4 5.4 collective-permute-start.12
  146.7 4.8 collective-permute-start.11
  214.9 13.1 %collective-permute-start.14 = (f32[1,1,6,32]{3,2,1,0:T(8,128)S(1)}, f32[1,1,6,32]{3,2,1,0:T(8,128)S(1)}, u32[]{:S(2)}, u32[]{:S(2)}) collective-permute-start(f32[1,1,6,32]{3,2,1,0:T(8,128)S(1)} %bitcast.399), channel_id=1, source_target_pairs={{4,0},{8,4},{12,8},{16,12},{20,16},{24,20},{28,24},{5,1},{9,5},{13... | collective-permute-start | bytes 2312 | tf_op jit(solution)/shard_map/ppermute | solution.py:26
  218.2 9.8 %collective-permute-start.13 = (f32[1,1,6,32]{3,2,1,0:T(8,128)S(1)}, f32[1,1,6,32]{3,2,1,0:T(8,128)S(1)}, u32[]{:S(2)}, u32[]{:S(2)}) collective-permute-start(f32[1,1,6,32]{3,2,1,0:T(8,128)S(1)} %bitcast.400), channel_id=1, source_target_pairs={{0,4},{4,8},{8,12},{12,16},{16,20},{20,24},{24,28},{1,5},{5,9},{9,... | collective-permute-start | bytes 2312 | tf_op jit(solution)/shard_map/ppermute | solution.py:24
  226.0 454.9 %collective-permute-start = (f32[512,512]{0,1:T(8,128)}, f32[512,512]{0,1:T(8,128)S(1)}, u32[]{:S(2)}, u32[]{:S(2)}) collective-permute-start(f32[512,512]{0,1:T(8,128)} %bitcast.3), channel_id=1, source_target_pairs={{4,0},{8,4},{12,8},{16,12},{20,16},{24,20},{28,24},{5,1},{9,5},{13... | collective-permute-start | bytes 3145736 | tf_op jit(solution)/shard_map/ppermute | solution.py:13
  228.0 6.6 collective-permute-start.16
  229.3 5.9 collective-permute-start.15
  298.0 85.4 %copy-start = (f32[2,1,512,512]{3,2,1,0:T(8,128)S(1)}, f32[2,1,512,512]{3,2,1,0:T(8,128)}, u32[]{:S(2)}) copy-start(f32[2,1,512,512]{3,2,1,0:T(8,128)} %param.14) | copy-start | bytes 6291460
  298.0 85.4 %copy-start.5 = (f32[2,1,32,512]{3,2,1,0:T(8,128)S(1)}, f32[2,1,32,512]{3,2,1,0:T(8,128)}, u32[]{:S(2)}) copy-start(f32[2,1,32,512]{3,2,1,0:T(8,128)} %param.16) | copy-start | bytes 393220
  298.0 163.4 %copy-start.6 = (f32[1,2,32,512]{3,2,1,0:T(8,128)S(1)}, f32[1,2,32,512]{3,2,1,0:T(8,128)}, u32[]{:S(2)}) copy-start(f32[1,2,32,512]{3,2,1,0:T(8,128)} %param.17) | copy-start | bytes 393220
  298.0 10.4 %collective-permute-start.18 = (f32[1,1,6,32]{3,2,1,0:T(8,128)S(1)}, f32[1,1,6,32]{3,2,1,0:T(8,128)S(1)}, u32[]{:S(2)}, u32[]{:S(2)}) collective-permute-start(f32[1,1,6,32]{3,2,1,0:T(8,128)S(1)} %bitcast.402), channel_id=1, source_target_pairs={{4,0},{8,4},{12,8},{16,12},{20,16},{24,20},{28,24},{5,1},{9,5},{13... | collective-permute-start | bytes 2312 | tf_op jit(solution)/shard_map/ppermute | solution.py:26
  301.5 6.9 collective-permute-start.17
  308.4 6.1 collective-permute-start.20
  309.7 5.5 collective-permute-start.19
  376.2 8.9 collective-permute-start.22
  379.5 5.5 collective-permute-start.21
  385.1 233.7 %copy-start.2 = (f32[1,1,512,512]{3,2,1,0:T(8,128)S(1)}, f32[1,1,512,512]{3,2,1,0:T(8,128)}, u32[]{:S(2)}) copy-start(f32[1,1,512,512]{3,2,1,0:T(8,128)} %get-tuple-element.82) | copy-start | bytes 3145732
  385.1 6.2 collective-permute-start.24
  386.5 5.5 collective-permute-start.23
  454.2 9.5 collective-permute-start.26
  457.6 6.1 collective-permute-start.25
  463.7 6.1 collective-permute-start.28
  465.0 5.5 collective-permute-start.27
  532.9 7.9 collective-permute-start.30
  536.2 4.5 collective-permute-start.29
  540.8 6.1 collective-permute-start.32
  542.1 5.5 collective-permute-start.31
  611.5 11.6 %collective-permute-start.34 = (f32[1,1,6,32]{3,2,1,0:T(8,128)S(1)}, f32[1,1,6,32]{3,2,1,0:T(8,128)S(1)}, u32[]{:S(2)}, u32[]{:S(2)}) collective-permute-start(f32[1,1,6,32]{3,2,1,0:T(8,128)S(1)} %bitcast.417), channel_id=1, source_target_pairs={{4,0},{8,4},{12,8},{16,12},{20,16},{24,20},{28,24},{5,1},{9,5},{13... | collective-permute-start | bytes 2312 | tf_op jit(solution)/shard_map/ppermute | solution.py:26
  614.9 9.5 collective-permute-start.33
  623.1 208.4 %collective-permute-start.37 = (f32[512,512]{0,1:T(8,128)}, f32[512,512]{0,1:T(8,128)}, u32[]{:S(2)}, u32[]{:S(2)}) collective-permute-start(f32[512,512]{0,1:T(8,128)} %bitcast.390), channel_id=1, source_target_pairs={{1,0},{2,1},{3,2},{5,4},{6,5},{7,6},{9,8},{10,9},{11,10},{13,12},{... | collective-permute-start | bytes 3145736 | tf_op jit(solution)/shard_map/ppermute | solution.py:13
  625.1 25.3 %collective-permute-start.36 = (f32[3,1,6,32]{3,2,1,0:T(8,128)S(1)}, f32[3,1,6,32]{3,2,1,0:T(8,128)S(1)}, u32[]{:S(2)}, u32[]{:S(2)}) collective-permute-start(f32[3,1,6,32]{3,2,1,0:T(8,128)S(1)} %pad_maximum_fusion.7), channel_id=1, source_target_pairs={{1,0},{2,1},{3,2},{5,4},{6,5},{7,6},{9,8},{10,9},{11,10},{13,12},{... | collective-permute-start | bytes 6920 | tf_op jit(solution)/shard_map/ppermute | solution.py:26
  650.4 4.4 collective-permute-start.35
  718.6 51.3 %copy-start.19 = (s32[4]{0:T(128)S(1)}, s32[4]{0:T(128)}, u32[]{:S(2)}) copy-start(s32[4]{0:T(128)} %iota_multiply_fusion) | copy-start | bytes 52
  770.7 60.8 %copy-start.1 = (f32[1,1,512,512]{2,3,1,0:T(8,128)S(1)}, f32[1,1,512,512]{2,3,1,0:T(8,128)}, u32[]{:S(2)}) copy-start(f32[1,1,512,512]{2,3,1,0:T(8,128)} %copy.41) | copy-start | bytes 3145732
  829.6 141.7 %collective-permute-start.2 = (f32[32,512]{1,0:T(8,128)}, f32[32,512]{1,0:T(8,128)}, u32[]{:S(2)}, u32[]{:S(2)}) collective-permute-start(f32[32,512]{1,0:T(8,128)} %get-tuple-element.75), channel_id=1, source_target_pairs={{0,4},{4,8},{8,12},{12,16},{16,20},{20,24},{24,28},{1,5},{5,9},{9,... | collective-permute-start | bytes 196616 | tf_op jit(solution)/shard_map/ppermute | solution.py:13
  917.3 54.9 %copy-start.9 = (f32[1,32,512]{2,1,0:T(8,128)S(1)}, f32[1,32,512]{2,1,0:T(8,128)}, u32[]{:S(2)}) copy-start(f32[1,32,512]{2,1,0:T(8,128)} %get-tuple-element.74) | copy-start | bytes 196612
  969.9 3.3 collective-permute-start.39
  (13 other events, 348.4 us)
